TPU v7x, 32 devices: a whole 2x2x4 slice. The times are simulated.
32 devices in a mesh: seq: 8 (over z, y), ctx: 4 (over x, core).
Axes of the slice: x: 2, y: 2, z: 4, core: 2. Of those that a mesh axis runs over, the one named last changes fastest.
Arguments:
- hidden_in: bfloat16 [8, 512, 1024], P('seq', 'ctx'), may hold values from -6 to 6
- positions: int32 [8, 512], P('seq', 'ctx'), may hold values from 0 to 499, as said below
- norm1_gain: float32 [1024], replicated, may hold values from 0.5 to 1.5
- w_query: bfloat16 [1024, 2048], P(('seq', 'ctx')), may hold values from -0.1875 to 0.1875
- key_weight_matrix: bfloat16 [1024, 1024], P(('seq', 'ctx')), may hold values from -0.1875 to 0.1875
- value_weight_matrix: bfloat16 [1024, 1024], P(('seq', 'ctx')), may hold values from -0.1875 to 0.1875
- query_gain: float32 [128], replicated, may hold values from 0.8 to 6
- key_gain: float32 [128], replicated, may hold values from 0.8 to 6
- w_out: bfloat16 [1024, 2048], P(('seq', 'ctx')), may hold values from -0.75 to 0.75
- norm2_gain: float32 [1024], replicated, may hold values from 0.5 to 1.5
- w_gate: bfloat16 [1024, 3072], P(('seq', 'ctx')), may hold values from -0.1875 to 0.1875
- w_up: bfloat16 [1024, 3072], P(('seq', 'ctx')), may hold values from -0.1875 to 0.1875
- w_down: bfloat16 [1024, 3072], P(('seq', 'ctx')), may hold values from -0.109375 to 0.109375
- cotangent: bfloat16 [8, 512, 1024], P('seq', 'ctx'), may hold values from -6 to 6
Outputs:
- out_hidden: bfloat16 [8, 512, 1024], P('seq', 'ctx')
- grad_hidden: bfloat16 [8, 512, 1024], P('seq', 'ctx')
- grad_query: float32 [1024, 2048], P(('seq', 'ctx'))
- grad_key: float32 [1024, 1024], P(('seq', 'ctx'))
- grad_value: float32 [1024, 1024], P(('seq', 'ctx'))
- grad_out: float32 [1024, 2048], P(('seq', 'ctx'))
- grad_gate: float32 [1024, 3072], P(('seq', 'ctx'))
- grad_up: float32 [1024, 3072], P(('seq', 'ctx'))
- grad_down: float32 [1024, 3072], P(('seq', 'ctx'))
- grad_norm1: float32 [1024], replicated
- grad_norm2: float32 [1024], replicated
- grad_query_gain: float32 [128], replicated
- grad_key_gain: float32 [128], replicated
Inputs may be any that keep to these rules, and one draw needn't show every extreme that they name: In each sequence positions are 0 at the first token and rise by one from token to token, except at the first token of a document, where they return to 0.
All inputs are finite; a program needn't handle non-finite values.
Results may differ from a plain program's by a relative error of at most 0.04.
The roundings to bfloat16 on the way count: a program that leaves them out, or rounds other values in their place, can miss the bound.
Values may be sent and summed in bfloat16 or wider, within the bound.
No kernel may reach another device: no remote copies, remote signals or barrier semaphores. Data moves between devices by JAX's collectives and lax.ppermute only.
A program may use at most 384 MiB of HBM per device.

v0:
```python
import functools

import jax
import jax.numpy as jnp
from jax import lax
from jax.experimental import pallas as pl
from jax.experimental.pallas import tpu as pltpu
from jax.sharding import PartitionSpec as P


NORM_EPSILON = 1e-06
ROPE_THETA = 1000000.0


def rope_tables(position_ids, head_width):
    half_width = head_width // 2
    inverse = ROPE_THETA ** (-(2.0 / head_width) * jnp.arange(half_width, dtype=jnp.float32))
    angles = position_ids.astype(jnp.float32)[:, None] * inverse[None, :]
    return (jnp.cos(angles), jnp.sin(angles))


def rotate(vectors, cosine, sine):
    half_width = vectors.shape[-1] // 2
    first = vectors[..., :half_width]
    second = vectors[..., half_width:]
    cos_rows = cosine[:, None, :]
    sin_rows = sine[:, None, :]
    return jnp.concatenate(
        (first * cos_rows - second * sin_rows, second * cos_rows + first * sin_rows), -1
    )


def rotate_back(grads, cosine, sine):
    half_width = grads.shape[-1] // 2
    first = grads[..., :half_width]
    second = grads[..., half_width:]
    cos_rows = cosine[:, None, :]
    sin_rows = sine[:, None, :]
    return jnp.concatenate(
        (first * cos_rows + second * sin_rows, second * cos_rows - first * sin_rows), -1
    )


def unit_rows(vectors):
    factor = lax.rsqrt(jnp.mean(vectors * vectors, -1, keepdims=True) + NORM_EPSILON)
    return (factor, vectors * factor)


def unit_back(grad_unit, factor, unit):
    return factor * (grad_unit - unit * jnp.mean(grad_unit * unit, -1, keepdims=True))


def outer_rows(left, right):
    return jnp.einsum("tj,tc->jc", left, right, preferred_element_type=jnp.float32)


def gathered_layer(
    hidden_in,
    positions,
    norm1_gain,
    w_query,
    key_weight_matrix,
    value_weight_matrix,
    query_gain,
    key_gain,
    w_out,
    norm2_gain,
    w_gate,
    w_up,
    w_down,
    cotangent,
):
    row_count = hidden_in.shape[1]
    head_width = query_gain.shape[0]
    query_columns = w_query.shape[1]
    key_value_columns = key_weight_matrix.shape[1]
    kv_heads = key_value_columns // head_width
    query_group_count = query_columns // key_value_columns
    attn_width = query_columns + 2 * key_value_columns + query_columns
    inputs = hidden_in[0].astype(jnp.float32)
    position_ids = positions[0]
    factor1, unit1 = unit_rows(inputs)
    normed1 = (unit1 * norm1_gain).astype(jnp.bfloat16)
    w_joint = jnp.concatenate((w_query, key_weight_matrix, value_weight_matrix), 1)
    joint_full, out_full = (
        lax.all_gather(w_joint, ("seq", "ctx"), axis=0, tiled=True),
        lax.all_gather(w_out, ("seq", "ctx"), axis=0, tiled=True),
    )
    projected_output = jnp.dot(normed1, joint_full, preferred_element_type=jnp.float32)
    query_raw = projected_output[:, :query_columns].reshape(
        row_count, query_columns // head_width, head_width
    )
    unrotated_key = projected_output[:, query_columns : query_columns + key_value_columns].reshape(
        row_count, kv_heads, head_width
    )
    unprojected_value = projected_output[:, query_columns + key_value_columns :].reshape(
        row_count, kv_heads, head_width
    )
    query_factor, query_unit = unit_rows(query_raw)
    key_factor, key_unit = unit_rows(unrotated_key)
    cosine, sine = rope_tables(position_ids, head_width)
    rotated_query = rotate(query_unit * query_gain, cosine, sine).astype(jnp.bfloat16)
    key_rot = rotate(key_unit * key_gain, cosine, sine).astype(jnp.bfloat16)
    query_head_rows = rotated_query.reshape(
        row_count, kv_heads, query_group_count, head_width
    ).transpose(1, 2, 0, 3)
    own_pair = jnp.stack((key_rot, unprojected_value.astype(jnp.bfloat16)))
    cycle_size = lax.axis_size("ctx")
    my_block = lax.axis_index("ctx")
    offsets = jnp.arange(row_count, dtype=jnp.int32)
    query_index = my_block * row_count + offsets
    doc_begin = query_index - position_ids
    score_scale = head_width ** (-0.5)

    def visible(count):
        key_index = jnp.arange(count, dtype=jnp.int32)
        return (key_index[None, :] <= query_index[:, None]) & (
            key_index[None, :] >= doc_begin[:, None]
        )

    def block_scores(key_value_couple, key_mask):
        scores = score_scale * jnp.einsum(
            "ekla,xea->eklx",
            query_head_rows,
            key_value_couple[0],
            preferred_element_type=jnp.float32,
        )
        return jnp.where(key_mask[None, None], scores, -jnp.inf)

    state = (
        jnp.full((kv_heads, query_group_count, row_count), -jnp.inf, jnp.float32),
        jnp.zeros((kv_heads, query_group_count, row_count), jnp.float32),
        jnp.zeros((kv_heads, query_group_count, row_count, head_width), jnp.float32),
    )
    key_value_couple = lax.all_gather(own_pair, "ctx", axis=1, tiled=True)
    key_mask = visible(key_value_couple.shape[1])

    def attend(current):
        highest, totals, accum = current
        scores = block_scores(key_value_couple, key_mask)
        new_high = jnp.max(scores, -1)
        decay = jnp.exp(highest - new_high)
        weights = jnp.exp(scores - new_high[..., None])
        totals = totals * decay + jnp.sum(weights, -1)
        accum = accum * decay[..., None] + jnp.einsum(
            "emaj,jep->emap",
            weights.astype(jnp.bfloat16),
            key_value_couple[1],
            preferred_element_type=jnp.float32,
        )
        return (new_high, totals, accum)

    highest, totals, accum = lax.cond(jnp.any(key_mask), attend, lambda current: current, state)
    log_total = highest + jnp.log(totals)
    attn_heads = (accum / totals[..., None]).astype(jnp.bfloat16)
    attention_row_block = attn_heads.transpose(2, 0, 1, 3).reshape(row_count, query_columns)
    attn_out = jnp.einsum(
        "tc,jc->tj", attention_row_block, out_full, preferred_element_type=jnp.float32
    )
    residual = inputs + attn_out
    factor2, unit2 = unit_rows(residual)
    normed2 = (unit2 * norm2_gain).astype(jnp.bfloat16)
    gate_full, up_full, down_full = (
        lax.all_gather(w_gate, ("seq", "ctx"), axis=0, tiled=True),
        lax.all_gather(w_up, ("seq", "ctx"), axis=0, tiled=True),
        lax.all_gather(w_down, ("seq", "ctx"), axis=0, tiled=True),
    )
    gate = jnp.dot(normed2, gate_full, preferred_element_type=jnp.float32)
    upward = jnp.dot(normed2, up_full, preferred_element_type=jnp.float32)
    sigmoid = jax.nn.sigmoid(gate)
    activation = gate * sigmoid
    hidden_units = (activation * upward).astype(jnp.bfloat16)
    mlp_out = jnp.einsum("tf,jf->tj", hidden_units, down_full, preferred_element_type=jnp.float32)
    out_hidden = (residual + mlp_out).astype(jnp.bfloat16)
    grad_out_b = cotangent[0]
    grad_hidden = jnp.dot(grad_out_b, down_full, preferred_element_type=jnp.float32)
    grad_gate = (grad_hidden * upward * sigmoid * (1.0 + gate * (1.0 - sigmoid))).astype(
        jnp.bfloat16
    )
    grad_up = (grad_hidden * activation).astype(jnp.bfloat16)
    grad_normed2 = jnp.einsum(
        "tf,jf->tj", grad_gate, gate_full, preferred_element_type=jnp.float32
    ) + jnp.einsum("tf,jf->tj", grad_up, up_full, preferred_element_type=jnp.float32)
    gain2_local = jnp.sum(grad_normed2 * unit2, 0)
    grad_residual = grad_out_b.astype(jnp.float32) + unit_back(
        grad_normed2 * norm2_gain, factor2, unit2
    )
    grad_residual_b = grad_residual.astype(jnp.bfloat16)
    grad_attn = jnp.dot(grad_residual_b, out_full, preferred_element_type=jnp.float32)
    attention_gradient_backward = grad_attn.astype(jnp.bfloat16)
    head_gradient = attention_gradient_backward.reshape(
        row_count, kv_heads, query_group_count, head_width
    ).transpose(1, 2, 0, 3)
    delta_rows = jnp.sum(head_gradient.astype(jnp.float32) * attn_heads.astype(jnp.float32), -1)
    grads_full = jnp.zeros((2, row_count * cycle_size, kv_heads, head_width), jnp.float32)
    grad_q_acc = jnp.zeros((kv_heads, query_group_count, row_count, head_width), jnp.float32)
    current = (grads_full, grad_q_acc)
    backward_key_value_couple = lax.all_gather(own_pair, "ctx", axis=1, tiled=True)
    piece_rows = backward_key_value_couple.shape[1]
    backward_key_mask = visible(piece_rows)

    def attend_back(inner):
        scores = block_scores(backward_key_value_couple, backward_key_mask)
        probs = jnp.exp(scores - log_total[..., None])
        probability_backward = probs.astype(jnp.bfloat16)
        grad_probs = jnp.einsum(
            "ekla,xea->eklx",
            head_gradient,
            backward_key_value_couple[1],
            preferred_element_type=jnp.float32,
        )
        score_gradient = (probs * (grad_probs - delta_rows[..., None])).astype(jnp.bfloat16)
        grad_q_acc = score_scale * jnp.einsum(
            "emaj,jep->emap",
            score_gradient,
            backward_key_value_couple[0],
            preferred_element_type=jnp.float32,
        )
        grad_keys = score_scale * jnp.einsum(
            "kejx,kejy->xky", score_gradient, query_head_rows, preferred_element_type=jnp.float32
        )
        grad_values = jnp.einsum(
            "kejx,kejy->xky",
            probability_backward,
            head_gradient,
            preferred_element_type=jnp.float32,
        )
        grads_full = jnp.stack((grad_keys, grad_values))
        return (grads_full, grad_q_acc)

    grads_full, grad_q_acc = lax.cond(
        jnp.any(backward_key_mask), attend_back, lambda inner: inner, current
    )
    grads_kv = lax.psum_scatter(
        grads_full.astype(jnp.bfloat16), "ctx", scatter_dimension=1, tiled=True
    ).astype(jnp.float32)
    grad_query = rotate_back(
        grad_q_acc.transpose(2, 0, 1, 3).reshape(
            row_count, query_columns // head_width, head_width
        ),
        cosine,
        sine,
    )
    grad_key = rotate_back(grads_kv[0], cosine, sine)
    qgain_local = jnp.sum(grad_query * query_unit, (0, 1))
    kgain_local = jnp.sum(grad_key * key_unit, (0, 1))
    grad_query_raw = unit_back(grad_query * query_gain, query_factor, query_unit)
    grad_key_raw = unit_back(grad_key * key_gain, key_factor, key_unit)
    grad_joint = jnp.concatenate(
        (
            grad_query_raw.reshape(row_count, query_columns),
            grad_key_raw.reshape(row_count, key_value_columns),
            grads_kv[1].reshape(row_count, key_value_columns),
        ),
        1,
    ).astype(jnp.bfloat16)
    grad_normed1 = jnp.einsum(
        "tc,jc->tj", grad_joint, joint_full, preferred_element_type=jnp.float32
    )
    gain1_local = jnp.sum(grad_normed1 * unit1, 0)
    grad_inputs = (grad_residual + unit_back(grad_normed1 * norm1_gain, factor1, unit1)).astype(
        jnp.bfloat16
    )
    joined = lax.psum_scatter(
        jnp.concatenate(
            (
                jnp.concatenate(
                    (
                        outer_rows(normed1, grad_joint),
                        outer_rows(grad_residual_b, attention_row_block),
                    ),
                    1,
                ),
                jnp.concatenate(
                    (
                        outer_rows(normed2, grad_gate),
                        outer_rows(normed2, grad_up),
                        outer_rows(grad_out_b, hidden_units),
                    ),
                    1,
                ),
            ),
            1,
        ),
        ("seq", "ctx"),
        scatter_dimension=0,
        tiled=True,
    )
    attn_grads = joined[:, :attn_width]
    mlp_grads = joined[:, attn_width:]
    gain_totals = lax.psum((gain1_local, gain2_local, qgain_local, kgain_local), ("seq", "ctx"))
    hidden_width = w_gate.shape[1]
    return (
        out_hidden[None],
        grad_inputs[None],
        attn_grads[:, :query_columns],
        attn_grads[:, query_columns : query_columns + key_value_columns],
        attn_grads[:, query_columns + key_value_columns : query_columns + 2 * key_value_columns],
        attn_grads[:, query_columns + 2 * key_value_columns :],
        mlp_grads[:, :hidden_width],
        mlp_grads[:, hidden_width : 2 * hidden_width],
        mlp_grads[:, 2 * hidden_width :],
        gain_totals[0],
        gain_totals[1],
        gain_totals[2],
        gain_totals[3],
    )


def turn(rows, cosine, sine):
    return rows * cosine + pltpu.roll(rows, rows.shape[-1] // 2, 1) * sine


def head_rows(raw, gain, cosine, sine):
    factor, unit = unit_rows(raw)
    return factor, unit, turn(unit * gain, cosine, sine).astype(jnp.bfloat16)


def dot_of(left, right, left_dim, right_dim):
    return lax.dot_general(
        left, right, (((left_dim,), (right_dim,)), ((), ())), preferred_element_type=jnp.float32
    )


def probabilities(key_rot, query_rot, mask):
    scores = dot_of(key_rot, query_rot, 1, 1) * key_rot.shape[-1] ** (-0.5) + mask
    weights = jnp.exp(scores - jnp.max(scores, 0, keepdims=True))
    return weights / jnp.sum(weights, 0, keepdims=True)


def attend_kernel(group, width, q_ref, k_ref, v_ref, mask_ref, cos_ref, sin_ref, qg_ref, kg_ref, o_ref):
    cosine, sine = cos_ref[...], sin_ref[...]
    key_rot = head_rows(k_ref[...], kg_ref[...], cosine, sine)[2]
    value = v_ref[...].astype(jnp.bfloat16)
    for r in range(group):
        cols = slice(r * width, (r + 1) * width)
        query_rot = head_rows(q_ref[:, cols], qg_ref[...], cosine, sine)[2]
        probs = probabilities(key_rot, query_rot, mask_ref[...]).astype(jnp.bfloat16)
        o_ref[:, cols] = dot_of(value, probs, 0, 0).T.astype(jnp.bfloat16)


def attend_back_kernel(
    group, width, q_ref, k_ref, v_ref, attn_ref, grad_ref, mask_ref, cos_ref, sin_ref,
    qg_ref, kg_ref, d_ref, gain_ref,
):
    cosine, sine = cos_ref[...], sin_ref[...]
    scale = width ** (-0.5)
    here = pl.program_id(0)
    kv_heads = pl.num_programs(0)

    def columns(head):
        return pl.ds(pl.multiple_of(head * width, width), width)

    key_factor, key_unit, key_rot = head_rows(k_ref[...], kg_ref[...], cosine, sine)
    value = v_ref[...].astype(jnp.bfloat16)

    @pl.when(pl.program_id(0) == 0)
    def _():
        gain_ref[...] = jnp.zeros_like(gain_ref)

    grad_key = jnp.zeros(key_rot.shape, jnp.float32)
    grad_value = jnp.zeros(key_rot.shape, jnp.float32)
    for r in range(group):
        cols = slice(r * width, (r + 1) * width)
        query_factor, query_unit, query_rot = head_rows(q_ref[:, cols], qg_ref[...], cosine, sine)
        probs = probabilities(key_rot, query_rot, mask_ref[...])
        grad = grad_ref[:, cols]
        product = grad.astype(jnp.float32) * attn_ref[:, cols].astype(jnp.float32)
        delta = jnp.sum(product.T, 0, keepdims=True)
        grad_scores = (probs * (dot_of(value, grad, 1, 1) - delta)).astype(jnp.bfloat16)
        grad_value += dot_of(probs.astype(jnp.bfloat16), grad, 1, 0)
        grad_key += dot_of(grad_scores, query_rot, 1, 0)
        grad_query = turn(scale * dot_of(key_rot, grad_scores, 0, 0).T, cosine, -sine)
        gain_ref[0:1, :] += jnp.sum(grad_query * query_unit, 0, keepdims=True)
        grad_query = unit_back(grad_query * qg_ref[...], query_factor, query_unit)
        d_ref[:, columns(here * group + r)] = grad_query.astype(jnp.bfloat16)
    grad_key = turn(scale * grad_key, cosine, -sine)
    gain_ref[1:2, :] += jnp.sum(grad_key * key_unit, 0, keepdims=True)
    grad_key = unit_back(grad_key * kg_ref[...], key_factor, key_unit)
    d_ref[:, columns(kv_heads * group + here)] = grad_key.astype(jnp.bfloat16)
    d_ref[:, columns(kv_heads * (group + 1) + here)] = grad_value.astype(jnp.bfloat16)


def attend_specs(tokens, width, heads, kv_heads):
    group = heads // kv_heads
    query = pl.BlockSpec((tokens, group * width), lambda h: (0, h))
    key = pl.BlockSpec((tokens, width), lambda h: (0, heads + h))
    value = pl.BlockSpec((tokens, width), lambda h: (0, heads + kv_heads + h))
    square = pl.BlockSpec((tokens, tokens), lambda h: (0, 0))
    table = pl.BlockSpec((tokens, width), lambda h: (0, 0))
    gain = pl.BlockSpec((1, width), lambda h: (0, 0))
    return query, key, value, square, table, gain


def attend(projected, mask, cosine, sine, gains, heads, kv_heads):
    tokens, width = cosine.shape
    query, key, value, square, table, gain = attend_specs(tokens, width, heads, kv_heads)
    return pl.pallas_call(
        functools.partial(attend_kernel, heads // kv_heads, width),
        grid=(kv_heads,),
        in_specs=[query, key, value, square, table, table, gain, gain],
        out_specs=query,
        out_shape=jax.ShapeDtypeStruct((tokens, heads * width), jnp.bfloat16),
        compiler_params=pltpu.CompilerParams(vmem_limit_bytes=16 << 20),
        name="attend",
    )(projected, projected, projected, mask, cosine, sine, *gains)


def attend_back(projected, attn, grad_attn, mask, cosine, sine, gains, heads, kv_heads):
    tokens, width = cosine.shape
    query, key, value, square, table, gain = attend_specs(tokens, width, heads, kv_heads)
    return pl.pallas_call(
        functools.partial(attend_back_kernel, heads // kv_heads, width),
        grid=(kv_heads,),
        in_specs=[query, key, value, query, query, square, table, table, gain, gain],
        out_specs=[
            pl.BlockSpec(projected.shape, lambda h: (0, 0)),
            pl.BlockSpec((8, width), lambda h: (0, 0)),
        ],
        out_shape=[
            jax.ShapeDtypeStruct(projected.shape, jnp.bfloat16),
            jax.ShapeDtypeStruct((8, width), jnp.float32),
        ],
        compiler_params=pltpu.CompilerParams(vmem_limit_bytes=24 << 20),
        name="attend_back",
    )(projected, projected, projected, attn, grad_attn, mask, cosine, sine, *gains)


def pack_kernel(count, *refs):
    matrices, out, sems = refs[:-2], refs[-2], refs[-1]
    copies = []
    start = 0
    for k, matrix in enumerate(matrices):
        n = matrix.shape[1] // count
        for d in range(count):
            copies.append(
                pltpu.make_async_copy(
                    matrix.at[:, d * n : (d + 1) * n],
                    out.at[d, :, start : start + n],
                    sems.at[k, d],
                )
            )
        start += n
    for copy in copies:
        copy.start()
    for copy in copies:
        copy.wait()


def pack(matrices, count):
    rows = matrices[0].shape[0]
    cols = sum(m.shape[1] for m in matrices) // count
    anywhere = pl.BlockSpec(memory_space=pl.ANY)
    return pl.pallas_call(
        functools.partial(pack_kernel, count),
        in_specs=[pl.BlockSpec(memory_space=pltpu.HBM)] * len(matrices),
        out_specs=anywhere,
        out_shape=jax.ShapeDtypeStruct((count, rows, cols), matrices[0].dtype),
        scratch_shapes=[pltpu.SemaphoreType.DMA((len(matrices), count))],
        name="pack",
    )(*matrices)


def unpack_kernel(sizes, pieces_ref, *outs):
    start = 0
    for out, n in zip(outs, sizes):
        for d in range(pieces_ref.shape[0]):
            piece = pieces_ref[d, :, start : start + n]
            out[:, d * n : (d + 1) * n] = piece.astype(jnp.float32)
        start += n


def unpack(pieces, sizes):
    count, rows, _ = pieces.shape
    return pl.pallas_call(
        functools.partial(unpack_kernel, tuple(sizes)),
        out_shape=[jax.ShapeDtypeStruct((rows, count * n), jnp.float32) for n in sizes],
        compiler_params=pltpu.CompilerParams(vmem_limit_bytes=8 << 20),
        name="unpack",
    )(pieces)


def can_slice(mesh):
    seq_size = mesh.shape["seq"]
    ctx_size = mesh.shape["ctx"]
    return seq_size == 8 and ctx_size == 4


def swap_ctx(array, bit, seq_size, ctx_size):
    pairs = [
        (s * ctx_size + c, s * ctx_size + (c ^ bit))
        for s in range(seq_size)
        for c in range(ctx_size)
    ]
    return lax.ppermute(array, ("seq", "ctx"), pairs)


def sliced_layer(*arrays):
    return sliced_body(*arrays)


def sliced_body(
    hidden_in,
    positions,
    norm1_gain,
    w_query,
    key_weight_matrix,
    value_weight_matrix,
    query_gain,
    key_gain,
    w_out,
    norm2_gain,
    w_gate,
    w_up,
    w_down,
    cotangent,
):
    seq_size = lax.axis_size("seq")
    ctx_size = lax.axis_size("ctx")
    my_seq = lax.axis_index("seq")
    my_ctx = lax.axis_index("ctx")
    row_count = hidden_in.shape[1]
    width = hidden_in.shape[2]
    head_width = query_gain.shape[0]
    heads = w_query.shape[1] // head_width // ctx_size
    kv_heads = key_weight_matrix.shape[1] // head_width // ctx_size
    hidden_cols = w_gate.shape[1] // ctx_size
    bits = [1 << b for b in reversed(range(ctx_size.bit_length() - 1))]
    block = width // seq_size
    half = seq_size // 2

    def spot_of(s):
        return jnp.where(s % 2 == 0, s // 2, seq_size - 1 - s // 2)

    ring = list(range(0, seq_size, 2)) + list(range(seq_size - 1, 0, -2))
    spot = spot_of(my_seq)
    offsets = [0]
    for k in range(1, half):
        offsets += [-k, k]
    offsets.append(half)
    place = {o % seq_size: k for k, o in enumerate(offsets)}
    order = []
    for o in offsets:
        r = (spot + (o + seq_size)) % seq_size
        order.append(jnp.where(r < half, 2 * r, 2 * (seq_size - 1 - r) + 1))
    unorder = []
    for s in range(seq_size):
        r = (ring.index(s) + seq_size - spot) % seq_size
        near = jnp.where(r < half, 2 * r, 2 * (seq_size - r) - 1)
        unorder.append(jnp.where(r == half, seq_size - 1, near))

    def pick_blocks(array, which):
        return jnp.concatenate(
            [
                lax.dynamic_slice_in_dim(array, which[k] * block, block, array.ndim - 1)
                for k in range(seq_size)
            ],
            array.ndim - 1,
        )

    def shift(array, by):
        pairs = [
            (
                ring[r] * ctx_size + c,
                ring[(r + by) % seq_size] * ctx_size + c,
            )
            for r in range(seq_size)
            for c in range(ctx_size)
        ]
        return lax.ppermute(array, ("seq", "ctx"), pairs)

    def swap(array, bit):
        return swap_ctx(array, bit, seq_size, ctx_size)

    def exchange(pieces):
        rest = pieces.shape[1:]
        state = pieces.reshape((2,) * len(bits) + rest)
        for axis, bit in enumerate(bits):
            mine = (my_ctx & bit) != 0
            low = lax.index_in_dim(state, 0, axis, False)
            high = lax.index_in_dim(state, 1, axis, False)
            keep = jnp.where(mine, high, low)
            got = swap(jnp.where(mine, low, high), bit)
            source = lax.broadcasted_iota(jnp.int32, state.shape, axis) == mine.astype(jnp.int32)
            state = jnp.where(source, jnp.expand_dims(keep, axis), jnp.expand_dims(got, axis))
        return state.reshape((ctx_size,) + rest)

    def join_tokens(array):
        for bit in bits:
            array = jnp.concatenate((array, swap(array, bit)), 0)
        return array

    def sum_tokens(array):
        for bit in reversed(bits):
            rows = array.shape[0] // 2
            got = swap(array[rows:].astype(jnp.bfloat16), bit)
            array = array[:rows] + got.astype(jnp.float32)
        return array

    def after(array, *others):
        return lax.optimization_barrier((array, *others))[0] if others else array

    def gather_rows(own, gates):
        blocks = [own]
        ahead = back = own
        for k in range(1, half):
            ahead = shift(ahead, 1)
            back = shift(back, -1)
            ahead, back = lax.optimization_barrier((ahead, back) + tuple(gates.get(k, ())))[:2]
            blocks += [ahead, back]
        middle = block // 2
        ahead = shift(ahead[:middle], 1)
        back = shift(back[middle:], -1)
        blocks.append(jnp.concatenate((ahead, back), 0))
        return blocks

    def scatter_rows(pairs):
        def rows_of(offset, sent):
            k = place[offset % seq_size]
            return jnp.concatenate(
                [dot(x[:, k * block : (k + 1) * block], after(g, *sent), first) for x, g in pairs],
                1,
            )

        middle = block // 2
        far = rows_of(half, ()).astype(jnp.bfloat16)
        sends = [(far[:middle], far[middle:])]
        for k in range(half - 1, -1, -1):
            ahead = shift(sends[-1][0], 1).astype(jnp.float32)
            back = shift(sends[-1][1], -1).astype(jnp.float32)
            if k == 0:
                total = rows_of(0, sends[-1]) + ahead + back
                return total.astype(jnp.bfloat16), sends
            to_ahead = rows_of(k, sends[-1])
            to_back = rows_of(-k, sends[-1])
            if k == half - 1:
                to_ahead = jnp.concatenate((to_ahead[:middle] + ahead, to_ahead[middle:]), 0)
                to_back = jnp.concatenate((to_back[:middle], to_back[middle:] + back), 0)
            else:
                to_ahead = to_ahead + ahead
                to_back = to_back + back
            sends.append(
                lax.optimization_barrier(
                    (to_ahead.astype(jnp.bfloat16), to_back.astype(jnp.bfloat16))
                )
            )

    def own_rows(matrices):
        return exchange(pack(matrices, ctx_size)).reshape(block, -1)

    def sum_all(array):
        for bit in reversed(bits):
            array = array + swap(array, bit)
        bit = 1
        while bit < seq_size:
            pairs = [
                (s * ctx_size + c, (s ^ bit) * ctx_size + c)
                for s in range(seq_size)
                for c in range(ctx_size)
            ]
            array = array + lax.ppermute(array, ("seq", "ctx"), pairs)
            bit *= 2
        return array

    def collect(rows, sizes):
        pieces = exchange(rows.reshape(ctx_size, -1, rows.shape[1]))
        return unpack(pieces, sizes)

    def dot(left, right, dims):
        return lax.dot_general(left, right, (dims, ((), ())), preferred_element_type=jnp.float32)

    plain = ((1,), (0,))
    last = ((1,), (1,))
    first = ((0,), (0,))

    gain1 = pick_blocks(norm1_gain, order)
    gain2 = pick_blocks(norm2_gain, order)
    inputs = pick_blocks(hidden_in[0], order).astype(jnp.float32)
    cot_own = pick_blocks(cotangent[0], order)
    factor1, unit1 = unit_rows(inputs)
    digits = jnp.where(
        jnp.arange(head_width)[None, :] < head_width // 2,
        positions[0][:, None] // 128,
        positions[0][:, None] % 128,
    ).astype(jnp.bfloat16)
    attn_own = own_rows([w_query, key_weight_matrix, value_weight_matrix, w_out])
    mlp_own = own_rows([w_gate, w_up, w_down])
    joined = join_tokens(
        jnp.concatenate(
            ((unit1 * gain1).astype(jnp.bfloat16), cot_own, digits), 1
        ),
    )
    normed1 = joined[:, :width]
    cot = joined[:, width : 2 * width]
    digits = joined[:, 2 * width :].astype(jnp.float32)
    position_ids = (digits[:, 0] * 128.0 + digits[:, head_width // 2]).astype(jnp.int32)

    query_cols = heads * head_width
    kv_cols = kv_heads * head_width
    owners = [0]
    for bit in bits:
        owners = owners + [o ^ bit for o in owners]
    index = jnp.concatenate(
        [(my_ctx ^ o) * row_count + jnp.arange(row_count, dtype=jnp.int32) for o in owners]
    )
    begin = index - position_ids
    allowed = (index[:, None] <= index[None, :]) & (index[:, None] >= begin[None, :])
    mask = jnp.where(allowed, 0.0, -jnp.inf)
    cosine, sine = rope_tables(position_ids, head_width)
    cosine = jnp.concatenate((cosine, cosine), 1)
    sine = jnp.concatenate((-sine, sine), 1)

    attn_blocks = gather_rows(attn_own, {half - 1: (mask, cosine, sine)})
    mlp_blocks = gather_rows(mlp_own, {})
    attn_full = jnp.concatenate(attn_blocks, 0)
    mlp_full = jnp.concatenate(mlp_blocks, 0)
    joint = attn_full[:, : query_cols + 2 * kv_cols]
    out_cols = attn_full[:, query_cols + 2 * kv_cols :]
    gate_up = mlp_full[:, : 2 * hidden_cols]
    down = mlp_full[:, 2 * hidden_cols :]

    projected = dot(normed1, joint, plain)
    gains = (query_gain[None, :], key_gain[None, :])
    attn = attend(projected, mask, cosine, sine, gains, heads, kv_heads)

    residual = inputs + sum_tokens(dot(attn, out_cols, last))
    factor2, unit2 = unit_rows(residual)
    normed2 = join_tokens((unit2 * gain2).astype(jnp.bfloat16))
    gate_up_out = dot(normed2, gate_up, plain)
    gate = gate_up_out[:, :hidden_cols]
    upward = gate_up_out[:, hidden_cols:]
    sigmoid = jax.nn.sigmoid(gate)
    activation = gate * sigmoid
    hidden_units = (activation * upward).astype(jnp.bfloat16)
    grad_hid = dot(cot, down, plain)
    grad_gate = grad_hid * upward * sigmoid * (1.0 + gate * (1.0 - sigmoid))
    grad_up = grad_hid * activation
    grad_gate_up = jnp.concatenate((grad_gate, grad_up), 1).astype(jnp.bfloat16)
    back_mlp = dot(grad_gate_up, gate_up, last)
    grad_normed2 = sum_tokens(back_mlp)
    gain2_local = jnp.sum(grad_normed2 * unit2, 0)
    grad_residual = cot_own.astype(jnp.float32) + unit_back(grad_normed2 * gain2, factor2, unit2)
    grad_residual_b = join_tokens(grad_residual.astype(jnp.bfloat16))
    grad_attn = dot(grad_residual_b, out_cols, plain).astype(jnp.bfloat16)
    mlp_rows, _ = scatter_rows([(cot, hidden_units), (normed2, grad_gate_up)])
    grad_joint, gain_local = attend_back(
        projected, attn, grad_attn, mask, cosine, sine, gains, heads, kv_heads
    )
    grad_down_w, grad_gate_w, grad_up_w = collect(mlp_rows, [hidden_cols] * 3)
    attn_rows, sends = scatter_rows([(grad_residual_b, attn), (normed1, grad_joint)])
    grad_out_w, grad_query_w, grad_key_w, grad_value_w = collect(
        attn_rows, [query_cols, query_cols, kv_cols, kv_cols]
    )
    late_units = after(hidden_units, *sends[2])
    late_out = dot(late_units, down, last)
    out_hidden = (residual + sum_tokens(late_out)).astype(jnp.bfloat16)

    back_joint = dot(grad_joint, joint, last)
    grad_normed1 = sum_tokens(back_joint)
    gain1_local = jnp.sum(grad_normed1 * unit1, 0)
    grad_inputs = (grad_residual + unit_back(grad_normed1 * gain1, factor1, unit1)).astype(
        jnp.bfloat16
    )
    gain_sizes = [width, width, head_width, head_width]
    gain_rows = sum_all(
        jnp.concatenate(
            (
                pick_blocks(gain1_local, unorder),
                pick_blocks(gain2_local, unorder),
                gain_local[0],
                gain_local[1],
            )
        ).reshape(-1, head_width),
    ).reshape(-1)
    gain_totals = []
    start = 0
    for n in gain_sizes:
        gain_totals.append(gain_rows[start : start + n])
        start += n
    return (
        pick_blocks(out_hidden, unorder)[None],
        pick_blocks(grad_inputs, unorder)[None],
        grad_query_w,
        grad_key_w,
        grad_value_w,
        grad_out_w,
        grad_gate_w,
        grad_up_w,
        grad_down_w,
        gain_totals[0],
        gain_totals[1],
        gain_totals[2],
        gain_totals[3],
    )


def solution(mesh):
    placed = (
        P("seq", "ctx", None),
        P("seq", "ctx"),
        P(),
        P(("seq", "ctx"), None),
        P(("seq", "ctx"), None),
        P(("seq", "ctx"), None),
        P(),
        P(),
        P(("seq", "ctx"), None),
        P(),
        P(("seq", "ctx"), None),
        P(("seq", "ctx"), None),
        P(("seq", "ctx"), None),
        P("seq", "ctx", None),
    )
    layer = sliced_layer if can_slice(mesh) else gathered_layer
    return jax.shard_map(
        layer,
        mesh=mesh,
        in_specs=placed,
        out_specs=(
            P("seq", "ctx", None),
            P("seq", "ctx", None),
            P(("seq", "ctx"), None),
            P(("seq", "ctx"), None),
            P(("seq", "ctx"), None),
            P(("seq", "ctx"), None),
            P(("seq", "ctx"), None),
            P(("seq", "ctx"), None),
            P(("seq", "ctx"), None),
            P(),
            P(),
            P(),
            P(),
        ),
        check_vma=False,
    )
```

profile of v0, /device:TPU:0, one launch (start us, length us, event | category | flops | bytes accessed | tf_op | source)
XLA Modules:
  0.0 266.2 jit_solution(11905415104155849645)
XLA Ops:
  0.7 13.2 %pack.2 = bf16[4,32,1536]{2,1,0:T(8,128)(2,1)} custom-call(bf16[32,2048]{1,0:T(8,128)(2,1)} %refs_0_.2, bf16[32,1024]{1,0:T(8,128)(2,1)} %refs_1_.2, bf16[32,1024]{1,0:T(8,128)(2,1)} %refs_2_.2, bf16[32,2048]{1,0:T(8,128)(2,1)} %refs_3_.1), custom_call_target="tpu_custom_call" | custom-call | tf_op jit(solution)/shard_map/pack/pallas_call | solution.py:454
  14.9 3.0 %collective-permute-start.2 = (bf16[2,32,1536]{2,1,0:T(8,128)(2,1)S(1)}, bf16[2,32,1536]{2,1,0:T(8,128)(2,1)S(1)}, u32[]{:S(2)}, u32[]{:S(2)}) collective-permute-start(bf16[2,32,1536]{2,1,0:T(8,128)(2,1)S(1)} %get-tuple-element.143), channel_id=1, source_target_pairs={{0,2},{1,3},{2,0},{3,1},{4,6},{5,7},{6,4},{7,5},{8,10},{9,11},{10,... | collective-permute-start | bytes 589832 | tf_op jit(solution)/shard_map/ppermute | solution.py:495
  22.2 19.1 %pack.3 = bf16[4,32,2304]{2,1,0:T(8,128)(2,1)} custom-call(bf16[32,3072]{1,0:T(8,128)(2,1)} %refs_0_.3, bf16[32,3072]{1,0:T(8,128)(2,1)} %refs_1_.3, bf16[32,3072]{1,0:T(8,128)(2,1)} %refs_2_.3), custom_call_target="tpu_custom_call" | custom-call | tf_op jit(solution)/shard_map/pack/pallas_call | solution.py:454
  45.0 5.9 %collective-permute-done.16 = bf16[2,32,2304]{2,1,0:T(8,128)(2,1)S(1)} collective-permute-done((bf16[2,32,2304]{2,1,0:T(8,128)(2,1)S(1)}, bf16[2,32,2304]{2,1,0:T(8,128)(2,1)S(1)}, u32[]{:S(2)}, u32[]{:S(2)}) %collective-permute-start.16) | collective-permute-done | bytes 294944 | tf_op jit(solution)/shard_map/ppermute | solution.py:495
  57.6 7.1 %collective-permute-done.4 = bf16[128,1536]{1,0:T(8,128)(2,1)S(1)} collective-permute-done((bf16[128,1536]{1,0:T(8,128)(2,1)S(1)}, bf16[128,1536]{1,0:T(8,128)(2,1)S(1)}, u32[]{:S(2)}, u32[]{:S(2)}) %collective-permute-start.4) | collective-permute-done | bytes 393248 | tf_op jit(solution)/shard_map/ppermute | solution.py:570
  68.5 16.9 %collective-permute-done.6 = bf16[128,1536]{1,0:T(8,128)(2,1)S(1)} collective-permute-done((bf16[128,1536]{1,0:T(8,128)(2,1)S(1)}, bf16[128,1536]{1,0:T(8,128)(2,1)S(1)}, u32[]{:S(2)}, u32[]{:S(2)}) %collective-permute-start.6) | collective-permute-done | bytes 393248 | tf_op jit(solution)/shard_map/ppermute | solution.py:570
  93.1 5.6 %collective-permute-done.8 = bf16[128,1536]{1,0:T(8,128)(2,1)S(1)} collective-permute-done((bf16[128,1536]{1,0:T(8,128)(2,1)S(1)}, bf16[128,1536]{1,0:T(8,128)(2,1)S(1)}, u32[]{:S(2)}, u32[]{:S(2)}) %collective-permute-start.8) | collective-permute-done | bytes 393248 | tf_op jit(solution)/shard_map/ppermute | solution.py:570
  102.5 8.8 %collective-permute-done.20 = bf16[128,2304]{1,0:T(8,128)(2,1)S(1)} collective-permute-done((bf16[128,2304]{1,0:T(8,128)(2,1)S(1)}, bf16[128,2304]{1,0:T(8,128)(2,1)S(1)}, u32[]{:S(2)}, u32[]{:S(2)}) %collective-permute-start.20) | collective-permute-done | bytes 589856 | tf_op jit(solution)/shard_map/ppermute | solution.py:570
  118.4 5.0 %attend.1.attn_ref = bf16[512,512]{1,0:T(8,128)(2,1)S(1)} custom-call(f32[512,1024]{1,0:T(8,128)S(1)} %fusion.6.q_ref.k_ref.v_ref, f32[512,1024]{1,0:T(8,128)S(1)} %fusion.6.q_ref.k_ref.v_ref, f32[512,1024]{1,0:T(8,128)S(1)} %fusion.6.q_ref.k_ref.v_ref, f32[512,512]{1,0:T(8,128)S(1)} %and_select_fusion.mask_ref, f32[512,128]{1,0:T(8,128)S(1)} %pad_maximum_fusion.16.cos_ref, ...), custom_call_target="tpu_custom_call" | custom-call | tf_op jit(solution)/shard_map/attend/pallas_call | solution.py:398
  124.4 2.2 collective-permute-done.22
  131.3 5.6 %collective-permute-done.13 = bf16[128,1024]{1,0:T(8,128)(2,1)S(1)} collective-permute-done((bf16[128,1024]{1,0:T(8,128)(2,1)S(1)}, bf16[128,1024]{1,0:T(8,128)(2,1)S(1)}, u32[]{:S(2)}, u32[]{:S(2)}) %collective-permute-start.13) | collective-permute-done | bytes 262176 | tf_op jit(solution)/shard_map/ppermute | solution.py:495
  139.7 4.1 %collective-permute-done.14 = bf16[128,1024]{1,0:T(8,128)(2,1)S(1)} collective-permute-done((bf16[128,1024]{1,0:T(8,128)(2,1)S(1)}, bf16[128,1024]{1,0:T(8,128)(2,1)S(1)}, u32[]{:S(2)}, u32[]{:S(2)}) %collective-permute-start.14) | collective-permute-done | bytes 262176 | tf_op jit(solution)/shard_map/ppermute | solution.py:495
  155.8 5.2 %collective-permute-done.44 = bf16[64,2304]{1,0:T(8,128)(2,1)S(1)} collective-permute-done((bf16[64,2304]{1,0:T(8,128)(2,1)S(1)}, bf16[64,2304]{1,0:T(8,128)(2,1)S(1)}, u32[]{:S(2)}, u32[]{:S(2)}) %collective-permute-start.44) | collective-permute-done | bytes 294944 | tf_op jit(solution)/shard_map/ppermute | solution.py:570
  168.2 4.4 %collective-permute-done.27 = bf16[128,1024]{1,0:T(8,128)(2,1)S(1)} collective-permute-done((bf16[128,1024]{1,0:T(8,128)(2,1)S(1)}, bf16[128,1024]{1,0:T(8,128)(2,1)S(1)}, u32[]{:S(2)}, u32[]{:S(2)}) %collective-permute-start.27) | collective-permute-done | bytes 262176 | tf_op jit(solution)/shard_map/ppermute | solution.py:495
  174.8 2.3 collective-permute-done.46
  181.2 9.4 %collective-permute-done.48 = bf16[128,2304]{1,0:T(8,128)(2,1)S(1)} collective-permute-done((bf16[128,2304]{1,0:T(8,128)(2,1)S(1)}, bf16[128,2304]{1,0:T(8,128)(2,1)S(1)}, u32[]{:S(2)}, u32[]{:S(2)}) %collective-permute-start.48) | collective-permute-done | bytes 589856 | tf_op jit(solution)/shard_map/ppermute | solution.py:570
  195.8 7.1 %attend_back.1 = (bf16[512,1024]{1,0:T(8,128)(2,1)S(1)}, f32[8,128]{1,0:T(8,128)S(1)}) custom-call(f32[512,1024]{1,0:T(8,128)S(1)} %fusion.6.q_ref.k_ref.v_ref, f32[512,1024]{1,0:T(8,128)S(1)} %fusion.6.q_ref.k_ref.v_ref, f32[512,1024]{1,0:T(8,128)S(1)} %fusion.6.q_ref.k_ref.v_ref, bf16[512,512]{1,0:T(8,128)(2,1)S(1)} %attend.1.attn_ref, ...), custom_call_target="tpu_custom_call" | custom-call | tf_op jit(solution)/shard_map/attend_back/pallas_call | solution.py:412
  217.1 3.2 %collective-permute-done.32 = bf16[128,1536]{1,0:T(8,128)(2,1)S(1)} collective-permute-done((bf16[128,1536]{1,0:T(8,128)(2,1)S(1)}, bf16[128,1536]{1,0:T(8,128)(2,1)S(1)}, u32[]{:S(2)}, u32[]{:S(2)}) %collective-permute-start.32) | collective-permute-done | bytes 393248 | tf_op jit(solution)/shard_map/ppermute | solution.py:570
  231.8 2.1 collective-permute-done.55
  235.4 2.1 collective-permute-done.56
  238.5 2.7 %collective-permute-done.57 = f32[18,128]{1,0:T(8,128)S(1)} collective-permute-done((f32[18,128]{1,0:T(8,128)S(1)}, f32[18,128]{1,0:T(8,128)S(1)}, u32[]{:S(2)}, u32[]{:S(2)}) %collective-permute-start.57) | collective-permute-done | bytes 9248 | tf_op jit(solution)/shard_map/ppermute | solution.py:661
  243.1 2.7 %collective-permute-done.58 = f32[18,128]{1,0:T(8,128)S(1)} collective-permute-done((f32[18,128]{1,0:T(8,128)S(1)}, f32[18,128]{1,0:T(8,128)S(1)}, u32[]{:S(2)}, u32[]{:S(2)}) %collective-permute-start.58) | collective-permute-done | bytes 9248 | tf_op jit(solution)/shard_map/ppermute | solution.py:661
  252.9 3.2 %collective-permute-done.35 = bf16[128,1024]{1,0:T(8,128)(2,1)S(1)} collective-permute-done((bf16[128,1024]{1,0:T(8,128)(2,1)S(1)}, bf16[128,1024]{1,0:T(8,128)(2,1)S(1)}, u32[]{:S(2)}, u32[]{:S(2)}) %collective-permute-start.35) | collective-permute-done | bytes 262176 | tf_op jit(solution)/shard_map/ppermute | solution.py:495
  259.6 4.0 %collective-permute-done.42 = bf16[2,32,1536]{2,1,0:T(8,128)(2,1)S(1)} collective-permute-done((bf16[2,32,1536]{2,1,0:T(8,128)(2,1)S(1)}, bf16[2,32,1536]{2,1,0:T(8,128)(2,1)S(1)}, u32[]{:S(2)}, u32[]{:S(2)}) %collective-permute-start.42) | collective-permute-done | bytes 196640 | tf_op jit(solution)/shard_map/ppermute | solution.py:495
  (348 shorter events, 119.2 us)
Async XLA Ops:
  14.9 29.9 %collective-permute-start.2 = (bf16[2,32,1536]{2,1,0:T(8,128)(2,1)S(1)}, bf16[2,32,1536]{2,1,0:T(8,128)(2,1)S(1)}, u32[]{:S(2)}, u32[]{:S(2)}) collective-permute-start(bf16[2,32,1536]{2,1,0:T(8,128)(2,1)S(1)} %get-tuple-element.143), channel_id=1, source_target_pairs={{0,2},{1,3},{2,0},{3,1},{4,6},{5,7},{6,4},{7,5},{8,10},{9,11},{10,... | collective-permute-start | bytes 589832 | tf_op jit(solution)/shard_map/ppermute | solution.py:495
  21.9 35.6 %collective-permute-start = (bf16[128,2176]{1,0:T(8,128)(2,1)S(1)}, bf16[128,2176]{1,0:T(8,128)(2,1)S(1)}, u32[]{:S(2)}, u32[]{:S(2)}) collective-permute-start(bf16[128,2176]{1,0:T(8,128)(2,1)S(1)} %constant_dynamic-update-slice_fusion.9), channel_id=1, source_target_pairs={{0,2},{1,3},{2,0},{3,1},{4,6},{5,7},{6,4},{7,5},{8,10},{9,11},{10,... | collective-permute-start | bytes 1671176 | tf_op jit(solution)/shard_map/ppermute | solution.py:495
  55.4 33.3 %collective-permute-start.18 = (bf16[128,2304]{1,0:T(8,128)(2,1)S(1)}, bf16[128,2304]{1,0:T(8,128)(2,1)S(1)}, u32[]{:S(2)}, u32[]{:S(2)}) collective-permute-start(bf16[128,2304]{1,0:T(8,128)(2,1)S(1)} %get-tuple-element.170), channel_id=1, source_target_pairs={{0,8},{1,9},{2,10},{3,11},{8,16},{9,17},{10,18},{11,19},{16,24},{1... | collective-permute-start | bytes 1769480 | tf_op jit(solution)/shard_map/ppermute | solution.py:570
  57.0 31.7 %collective-permute-start.19 = (bf16[128,2304]{1,0:T(8,128)(2,1)S(1)}, bf16[128,2304]{1,0:T(8,128)(2,1)S(1)}, u32[]{:S(2)}, u32[]{:S(2)}) collective-permute-start(bf16[128,2304]{1,0:T(8,128)(2,1)S(1)} %get-tuple-element.170), channel_id=1, source_target_pairs={{0,4},{1,5},{2,6},{3,7},{8,0},{9,1},{10,2},{11,3},{16,8},{17,9},{1... | collective-permute-start | bytes 1769480 | tf_op jit(solution)/shard_map/ppermute | solution.py:570
  57.6 33.4 %collective-permute-start.1 = (bf16[256,2176]{1,0:T(8,128)(2,1)S(1)}, bf16[256,2176]{1,0:T(8,128)(2,1)S(1)}, u32[]{:S(2)}, u32[]{:S(2)}) collective-permute-start(bf16[256,2176]{1,0:T(8,128)(2,1)S(1)} %pad_maximum_fusion.2), channel_id=1, source_target_pairs={{0,1},{1,0},{2,3},{3,2},{4,5},{5,4},{6,7},{7,6},{8,9},{9,8},{10,11... | collective-permute-start | bytes 3342344 | tf_op jit(solution)/shard_map/ppermute | solution.py:495
  66.4 19.0 %collective-permute-start.6 = (bf16[128,1536]{1,0:T(8,128)(2,1)S(1)}, bf16[128,1536]{1,0:T(8,128)(2,1)S(1)}, u32[]{:S(2)}, u32[]{:S(2)}) collective-permute-start(bf16[128,1536]{1,0:T(8,128)(2,1)S(1)} %collective-permute-done.4), channel_id=1, source_target_pairs={{0,8},{1,9},{2,10},{3,11},{8,16},{9,17},{10,18},{11,19},{16,24},{1... | collective-permute-start | bytes 1179656 | tf_op jit(solution)/shard_map/ppermute | solution.py:570
  68.0 18.8 %collective-permute-start.7 = (bf16[128,1536]{1,0:T(8,128)(2,1)S(1)}, bf16[128,1536]{1,0:T(8,128)(2,1)S(1)}, u32[]{:S(2)}, u32[]{:S(2)}) collective-permute-start(bf16[128,1536]{1,0:T(8,128)(2,1)S(1)} %collective-permute-done.5), channel_id=1, source_target_pairs={{0,4},{1,5},{2,6},{3,7},{8,0},{9,1},{10,2},{11,3},{16,8},{17,9},{1... | collective-permute-start | bytes 1179656 | tf_op jit(solution)/shard_map/ppermute | solution.py:570
  88.7 22.6 %collective-permute-start.20 = (bf16[128,2304]{1,0:T(8,128)(2,1)S(1)}, bf16[128,2304]{1,0:T(8,128)(2,1)S(1)}, u32[]{:S(2)}, u32[]{:S(2)}) collective-permute-start(bf16[128,2304]{1,0:T(8,128)(2,1)S(1)} %collective-permute-done.18), channel_id=1, source_target_pairs={{0,8},{1,9},{2,10},{3,11},{8,16},{9,17},{10,18},{11,19},{16,24},{1... | collective-permute-start | bytes 1769480 | tf_op jit(solution)/shard_map/ppermute | solution.py:570
  90.3 22.6 %collective-permute-start.21 = (bf16[128,2304]{1,0:T(8,128)(2,1)S(1)}, bf16[128,2304]{1,0:T(8,128)(2,1)S(1)}, u32[]{:S(2)}, u32[]{:S(2)}) collective-permute-start(bf16[128,2304]{1,0:T(8,128)(2,1)S(1)} %collective-permute-done.19), channel_id=1, source_target_pairs={{0,4},{1,5},{2,6},{3,7},{8,0},{9,1},{10,2},{11,3},{16,8},{17,9},{1... | collective-permute-start | bytes 1769480 | tf_op jit(solution)/shard_map/ppermute | solution.py:570
  100.3 15.3 %collective-permute-start.10 = (bf16[64,1536]{1,0:T(8,128)(2,1)S(1)}, bf16[64,1536]{1,0:T(8,128)(2,1)S(1)}, u32[]{:S(2)}, u32[]{:S(2)}) collective-permute-start(bf16[64,1536]{1,0:T(8,128)(2,1)S(1)} %slice.347), channel_id=1, source_target_pairs={{0,8},{1,9},{2,10},{3,11},{8,16},{9,17},{10,18},{11,19},{16,24},{1... | collective-permute-start | bytes 589832 | tf_op jit(solution)/shard_map/ppermute | solution.py:570
  101.9 15.2 %collective-permute-start.11 = (bf16[64,1536]{1,0:T(8,128)(2,1)S(1)}, bf16[64,1536]{1,0:T(8,128)(2,1)S(1)}, u32[]{:S(2)}, u32[]{:S(2)}) collective-permute-start(bf16[64,1536]{1,0:T(8,128)(2,1)S(1)} %slice.348), channel_id=1, source_target_pairs={{0,4},{1,5},{2,6},{3,7},{8,0},{9,1},{10,2},{11,3},{16,8},{17,9},{1... | collective-permute-start | bytes 589832 | tf_op jit(solution)/shard_map/ppermute | solution.py:570
  112.9 13.7 %collective-permute-start.22 = (bf16[128,2304]{1,0:T(8,128)(2,1)S(1)}, bf16[128,2304]{1,0:T(8,128)(2,1)S(1)}, u32[]{:S(2)}, u32[]{:S(2)}) collective-permute-start(bf16[128,2304]{1,0:T(8,128)(2,1)S(1)} %collective-permute-done.20), channel_id=1, source_target_pairs={{0,8},{1,9},{2,10},{3,11},{8,16},{9,17},{10,18},{11,19},{16,24},{1... | collective-permute-start | bytes 1769480 | tf_op jit(solution)/shard_map/ppermute | solution.py:570
  114.5 13.4 %collective-permute-start.23 = (bf16[128,2304]{1,0:T(8,128)(2,1)S(1)}, bf16[128,2304]{1,0:T(8,128)(2,1)S(1)}, u32[]{:S(2)}, u32[]{:S(2)}) collective-permute-start(bf16[128,2304]{1,0:T(8,128)(2,1)S(1)} %collective-permute-done.21), channel_id=1, source_target_pairs={{0,4},{1,5},{2,6},{3,7},{8,0},{9,1},{10,2},{11,3},{16,8},{17,9},{1... | collective-permute-start | bytes 1769480 | tf_op jit(solution)/shard_map/ppermute | solution.py:570
  127.9 16.0 %collective-permute-start.24 = (bf16[64,2304]{1,0:T(8,128)(2,1)S(1)}, bf16[64,2304]{1,0:T(8,128)(2,1)S(1)}, u32[]{:S(2)}, u32[]{:S(2)}) collective-permute-start(bf16[64,2304]{1,0:T(8,128)(2,1)S(1)} %slice.359), channel_id=1, source_target_pairs={{0,8},{1,9},{2,10},{3,11},{8,16},{9,17},{10,18},{11,19},{16,24},{1... | collective-permute-start | bytes 884744 | tf_op jit(solution)/shard_map/ppermute | solution.py:570
  163.0 14.1 %collective-permute-start.46 = (bf16[128,2304]{1,0:T(8,128)(2,1)S(1)}, bf16[128,2304]{1,0:T(8,128)(2,1)S(1)}, u32[]{:S(2)}, u32[]{:S(2)}) collective-permute-start(bf16[128,2304]{1,0:T(8,128)(2,1)S(1)} %pad_maximum_fusion.7), channel_id=1, source_target_pairs={{0,8},{1,9},{2,10},{3,11},{8,16},{9,17},{10,18},{11,19},{16,24},{1... | collective-permute-start | bytes 1769480 | tf_op jit(solution)/shard_map/ppermute | solution.py:570
  163.6 13.8 %collective-permute-start.47 = (bf16[128,2304]{1,0:T(8,128)(2,1)S(1)}, bf16[128,2304]{1,0:T(8,128)(2,1)S(1)}, u32[]{:S(2)}, u32[]{:S(2)}) collective-permute-start(bf16[128,2304]{1,0:T(8,128)(2,1)S(1)} %pad_maximum_fusion.8), channel_id=1, source_target_pairs={{0,4},{1,5},{2,6},{3,7},{8,0},{9,1},{10,2},{11,3},{16,8},{17,9},{1... | collective-permute-start | bytes 1769480 | tf_op jit(solution)/shard_map/ppermute | solution.py:570
  177.5 13.1 %collective-permute-start.48 = (bf16[128,2304]{1,0:T(8,128)(2,1)S(1)}, bf16[128,2304]{1,0:T(8,128)(2,1)S(1)}, u32[]{:S(2)}, u32[]{:S(2)}) collective-permute-start(bf16[128,2304]{1,0:T(8,128)(2,1)S(1)} %fusion.13), channel_id=1, source_target_pairs={{0,8},{1,9},{2,10},{3,11},{8,16},{9,17},{10,18},{11,19},{16,24},{1... | collective-permute-start | bytes 1769480 | tf_op jit(solution)/shard_map/ppermute | solution.py:570
  178.8 13.4 %collective-permute-start.49 = (bf16[128,2304]{1,0:T(8,128)(2,1)S(1)}, bf16[128,2304]{1,0:T(8,128)(2,1)S(1)}, u32[]{:S(2)}, u32[]{:S(2)}) collective-permute-start(bf16[128,2304]{1,0:T(8,128)(2,1)S(1)} %fusion.14), channel_id=1, source_target_pairs={{0,4},{1,5},{2,6},{3,7},{8,0},{9,1},{10,2},{11,3},{16,8},{17,9},{1... | collective-permute-start | bytes 1769480 | tf_op jit(solution)/shard_map/ppermute | solution.py:570
  181.1 14.0 %collective-permute-start.29 = (bf16[256,1024]{1,0:T(8,128)(2,1)S(1)}, bf16[256,1024]{1,0:T(8,128)(2,1)S(1)}, u32[]{:S(2)}, u32[]{:S(2)}) collective-permute-start(bf16[256,1024]{1,0:T(8,128)(2,1)S(1)} %pad_maximum_fusion.10), channel_id=1, source_target_pairs={{0,1},{1,0},{2,3},{3,2},{4,5},{5,4},{6,7},{7,6},{8,9},{9,8},{10,11... | collective-permute-start | bytes 1572872 | tf_op jit(solution)/shard_map/ppermute | solution.py:495
  192.3 22.2 %collective-permute-start.51 = (bf16[128,2304]{1,0:T(8,128)(2,1)S(1)}, bf16[128,2304]{1,0:T(8,128)(2,1)S(1)}, u32[]{:S(2)}, u32[]{:S(2)}) collective-permute-start(bf16[128,2304]{1,0:T(8,128)(2,1)S(1)} %fusion.16), channel_id=1, source_target_pairs={{0,4},{1,5},{2,6},{3,7},{8,0},{9,1},{10,2},{11,3},{16,8},{17,9},{1... | collective-permute-start | bytes 1769480 | tf_op jit(solution)/shard_map/ppermute | solution.py:570
  193.9 20.6 %collective-permute-start.50 = (bf16[128,2304]{1,0:T(8,128)(2,1)S(1)}, bf16[128,2304]{1,0:T(8,128)(2,1)S(1)}, u32[]{:S(2)}, u32[]{:S(2)}) collective-permute-start(bf16[128,2304]{1,0:T(8,128)(2,1)S(1)} %fusion.15), channel_id=1, source_target_pairs={{0,8},{1,9},{2,10},{3,11},{8,16},{9,17},{10,18},{11,19},{16,24},{1... | collective-permute-start | bytes 1769480 | tf_op jit(solution)/shard_map/ppermute | solution.py:570
  221.1 25.8 %collective-permute-start.38 = (bf16[128,1536]{1,0:T(8,128)(2,1)S(1)}, bf16[128,1536]{1,0:T(8,128)(2,1)S(1)}, u32[]{:S(2)}, u32[]{:S(2)}) collective-permute-start(bf16[128,1536]{1,0:T(8,128)(2,1)S(1)} %fusion.24), channel_id=1, source_target_pairs={{0,8},{1,9},{2,10},{3,11},{8,16},{9,17},{10,18},{11,19},{16,24},{1... | collective-permute-start | bytes 1179656 | tf_op jit(solution)/shard_map/ppermute | solution.py:570
  223.0 24.0 %collective-permute-start.39 = (bf16[128,1536]{1,0:T(8,128)(2,1)S(1)}, bf16[128,1536]{1,0:T(8,128)(2,1)S(1)}, u32[]{:S(2)}, u32[]{:S(2)}) collective-permute-start(bf16[128,1536]{1,0:T(8,128)(2,1)S(1)} %fusion.25), channel_id=1, source_target_pairs={{0,4},{1,5},{2,6},{3,7},{8,0},{9,1},{10,2},{11,3},{16,8},{17,9},{1... | collective-permute-start | bytes 1179656 | tf_op jit(solution)/shard_map/ppermute | solution.py:570
  224.8 24.6 %collective-permute-start.34 = (bf16[256,1024]{1,0:T(8,128)(2,1)S(1)}, bf16[256,1024]{1,0:T(8,128)(2,1)S(1)}, u32[]{:S(2)}, u32[]{:S(2)}) collective-permute-start(bf16[256,1024]{1,0:T(8,128)(2,1)S(1)} %slice.759), channel_id=1, source_target_pairs={{0,1},{1,0},{2,3},{3,2},{4,5},{5,4},{6,7},{7,6},{8,9},{9,8},{10,11... | collective-permute-start | bytes 1572872 | tf_op jit(solution)/shard_map/ppermute | solution.py:495
  (45 other events, 379.4 us)
where the time goes:
time: 267 us; the launch traced here: 266 us
  waiting for transfers between devices  121 us (45%)
  starting transfers between devices  57.3 us (21%)
  Pallas kernels  46.3 us (17%)
  matrix products  20.3 us (8%)
  other arithmetic  11.6 us (4%)
  local copies, waits for them, and re-layouts  7.95 us (3%)
    ppermute x32, waiting for transfers between devices, shift(): return lax.ppermute(array, ('seq', 'ctx'), pairs)  80.1 us
    ppermute x32, starting transfers between devices, shift(): return lax.ppermute(array, ('seq', 'ctx'), pairs)  33.6 us
    ppermute x24, waiting for transfers between devices, swap_ctx(): return lax.ppermute(array, ('seq', 'ctx'), pairs)  33.1 us
    pallas_call x2, Pallas kernels, pack(): pl.pallas_call(functools.partial(pack_kernel, count), in_specs=[pl.BlockS...  32.2 us
    dot_general x40, matrix products, dot(): lax.dot_general(left, right, (dims, ((), ())), preferred_element_type=jnp...  20.3 us
    ppermute x24, starting transfers between devices, swap_ctx(): return lax.ppermute(array, ('seq', 'ctx'), pairs)  19.4 us
    ppermute x3, waiting for transfers between devices, sum_all(): array = array + lax.ppermute(array, ('seq', 'ctx'), pairs)  7.55 us
    pallas_call x1, Pallas kernels, attend_back(): pl.pallas_call(functools.partial(attend_back_kernel, heads // kv_heads, w...  7.13 us
  transfers between devices with their start and end apart: 59, of which 37 were waited for; matrix products, arithmetic and copies ran while one was open for 12% of the time, Pallas kernels for 12%

commit v1 on v0

--- a/solution.py
+++ b/solution.py
@@ -426,37 +426,25 @@
     )(projected, projected, projected, attn, grad_attn, mask, cosine, sine, *gains)
 
 
-def pack_kernel(count, *refs):
-    matrices, out, sems = refs[:-2], refs[-2], refs[-1]
-    copies = []
+def pack_kernel(*refs):
+    out = refs[-1]
     start = 0
-    for k, matrix in enumerate(matrices):
-        n = matrix.shape[1] // count
-        for d in range(count):
-            copies.append(
-                pltpu.make_async_copy(
-                    matrix.at[:, d * n : (d + 1) * n],
-                    out.at[d, :, start : start + n],
-                    sems.at[k, d],
-                )
-            )
+    for matrix in refs[:-1]:
+        n = matrix.shape[1] // out.shape[0]
+        for d in range(out.shape[0]):
+            out[d, :, start : start + n] = matrix[:, d * n : (d + 1) * n]
         start += n
-    for copy in copies:
-        copy.start()
-    for copy in copies:
-        copy.wait()
 
 
 def pack(matrices, count):
     rows = matrices[0].shape[0]
     cols = sum(m.shape[1] for m in matrices) // count
-    anywhere = pl.BlockSpec(memory_space=pl.ANY)
     return pl.pallas_call(
-        functools.partial(pack_kernel, count),
-        in_specs=[pl.BlockSpec(memory_space=pltpu.HBM)] * len(matrices),
-        out_specs=anywhere,
+        pack_kernel,
+        grid=(1,),
+        in_specs=[pl.BlockSpec(m.shape, lambda i: (0, 0)) for m in matrices],
+        out_specs=pl.BlockSpec((count, rows, cols), lambda i: (0, 0, 0)),
         out_shape=jax.ShapeDtypeStruct((count, rows, cols), matrices[0].dtype),
-        scratch_shapes=[pltpu.SemaphoreType.DMA((len(matrices), count))],
         name="pack",
     )(*matrices)
 
@@ -639,14 +627,13 @@
             else:
                 to_ahead = to_ahead + ahead
                 to_back = to_back + back
-            sends.append(
-                lax.optimization_barrier(
-                    (to_ahead.astype(jnp.bfloat16), to_back.astype(jnp.bfloat16))
-                )
-            )
+            to_ahead = to_ahead.astype(jnp.bfloat16)
+            to_back = to_back.astype(jnp.bfloat16)
+            sends.append(lax.optimization_barrier((to_ahead, to_back)))
 
     def own_rows(matrices):
-        return exchange(pack(matrices, ctx_size)).reshape(block, -1)
+        pieces = pack(matrices, ctx_size)
+        return exchange(pieces).reshape(block, -1)
 
     def sum_all(array):
         for bit in reversed(bits):

time: 267 us -> 247 us (0.925)
  Pallas kernels: 46.3 us -> 17.9 us
  waiting for transfers between devices: 121 us -> 137 us
  starting transfers between devices: 57.3 us -> 49.7 us
    pallas_call x2, Pallas kernels: 32.2 us -> 3.86 us  [pack(): pl.pallas_call(pack_kernel, grid=(1,), in_specs=[pl.BlockSpec(m.shape, la...]
    ppermute x24, waiting for transfers between devices: 33.1 us -> 48.9 us  [swap_ctx(): return lax.ppermute(array, ('seq', 'ctx'), pairs)]
    ppermute x24, starting transfers between devices: 19.4 us -> 11.9 us  [swap_ctx(): return lax.ppermute(array, ('seq', 'ctx'), pairs)]
  transfers between devices with their start and end apart: 59 -> 59, of which waited for: 37 -> 38; matrix products, arithmetic and copies ran while one was open for 12% -> 13% of each run, Pallas kernels for 12% -> 6%
where the time goes in v1:
time: 247 us; the launch traced here: 246 us
  waiting for transfers between devices  137 us (55%)
  starting transfers between devices  49.7 us (20%)
  matrix products  20.2 us (8%)
  Pallas kernels  17.9 us (7%)
  other arithmetic  11.6 us (5%)
  local copies, waits for them, and re-layouts  7.95 us (3%)
    ppermute x32, waiting for transfers between devices, shift(): return lax.ppermute(array, ('seq', 'ctx'), pairs)  80.6 us
    ppermute x24, waiting for transfers between devices, swap_ctx(): return lax.ppermute(array, ('seq', 'ctx'), pairs)  48.9 us
    ppermute x32, starting transfers between devices, shift(): return lax.ppermute(array, ('seq', 'ctx'), pairs)  33.6 us
    dot_general x40, matrix products, dot(): lax.dot_general(left, right, (dims, ((), ())), preferred_element_type=jnp...  20.2 us
    ppermute x24, starting transfers between devices, swap_ctx(): return lax.ppermute(array, ('seq', 'ctx'), pairs)  11.9 us
    ppermute x3, waiting for transfers between devices, sum_all(): array = array + lax.ppermute(array, ('seq', 'ctx'), pairs)  7.54 us
    pallas_call x1, Pallas kernels, attend_back(): pl.pallas_call(functools.partial(attend_back_kernel, heads // kv_heads, w...  7.13 us
    unnamed x93, local copies, waits for them, and re-layouts  5.8 us
  transfers between devices with their start and end apart: 59, of which 38 were waited for; matrix products, arithmetic and copies ran while one was open for 13% of the time, Pallas kernels for 6%

profile of v1, /device:TPU:0, one launch (start us, length us, event | category | flops | bytes accessed | tf_op | source)
XLA Modules:
  0.0 246.5 jit_solution(5119650703612962743)
XLA Ops:
  0.7 1.9 pack.2
  3.6 3.0 %collective-permute-start.2 = (bf16[2,32,1536]{2,1,0:T(8,128)(2,1)S(1)}, bf16[2,32,1536]{2,1,0:T(8,128)(2,1)S(1)}, u32[]{:S(2)}, u32[]{:S(2)}) collective-permute-start(bf16[2,32,1536]{2,1,0:T(8,128)(2,1)S(1)} %get-tuple-element.143), channel_id=1, source_target_pairs={{0,2},{1,3},{2,0},{3,1},{4,6},{5,7},{6,4},{7,5},{8,10},{9,11},{10,... | collective-permute-start | bytes 589832 | tf_op jit(solution)/shard_map/ppermute | solution.py:483
  10.9 2.0 pack.3
  16.6 14.4 %collective-permute-done.16 = bf16[2,32,2304]{2,1,0:T(8,128)(2,1)S(1)} collective-permute-done((bf16[2,32,2304]{2,1,0:T(8,128)(2,1)S(1)}, bf16[2,32,2304]{2,1,0:T(8,128)(2,1)S(1)}, u32[]{:S(2)}, u32[]{:S(2)}) %collective-permute-start.16) | collective-permute-done | bytes 294944 | tf_op jit(solution)/shard_map/ppermute | solution.py:483
  37.8 7.1 %collective-permute-done.4 = bf16[128,1536]{1,0:T(8,128)(2,1)S(1)} collective-permute-done((bf16[128,1536]{1,0:T(8,128)(2,1)S(1)}, bf16[128,1536]{1,0:T(8,128)(2,1)S(1)}, u32[]{:S(2)}, u32[]{:S(2)}) %collective-permute-start.4) | collective-permute-done | bytes 393248 | tf_op jit(solution)/shard_map/ppermute | solution.py:558
  48.6 16.9 %collective-permute-done.6 = bf16[128,1536]{1,0:T(8,128)(2,1)S(1)} collective-permute-done((bf16[128,1536]{1,0:T(8,128)(2,1)S(1)}, bf16[128,1536]{1,0:T(8,128)(2,1)S(1)}, u32[]{:S(2)}, u32[]{:S(2)}) %collective-permute-start.6) | collective-permute-done | bytes 393248 | tf_op jit(solution)/shard_map/ppermute | solution.py:558
  73.2 5.6 %collective-permute-done.8 = bf16[128,1536]{1,0:T(8,128)(2,1)S(1)} collective-permute-done((bf16[128,1536]{1,0:T(8,128)(2,1)S(1)}, bf16[128,1536]{1,0:T(8,128)(2,1)S(1)}, u32[]{:S(2)}, u32[]{:S(2)}) %collective-permute-start.8) | collective-permute-done | bytes 393248 | tf_op jit(solution)/shard_map/ppermute | solution.py:558
  82.6 8.8 %collective-permute-done.20 = bf16[128,2304]{1,0:T(8,128)(2,1)S(1)} collective-permute-done((bf16[128,2304]{1,0:T(8,128)(2,1)S(1)}, bf16[128,2304]{1,0:T(8,128)(2,1)S(1)}, u32[]{:S(2)}, u32[]{:S(2)}) %collective-permute-start.20) | collective-permute-done | bytes 589856 | tf_op jit(solution)/shard_map/ppermute | solution.py:558
  98.5 5.0 %attend.1.attn_ref = bf16[512,512]{1,0:T(8,128)(2,1)S(1)} custom-call(f32[512,1024]{1,0:T(8,128)S(1)} %fusion.6.q_ref.k_ref.v_ref, f32[512,1024]{1,0:T(8,128)S(1)} %fusion.6.q_ref.k_ref.v_ref, f32[512,1024]{1,0:T(8,128)S(1)} %fusion.6.q_ref.k_ref.v_ref, f32[512,512]{1,0:T(8,128)S(1)} %and_select_fusion.mask_ref, f32[512,128]{1,0:T(8,128)S(1)} %pad_maximum_fusion.16.cos_ref, ...), custom_call_target="tpu_custom_call" | custom-call | tf_op jit(solution)/shard_map/attend/pallas_call | solution.py:398
  104.5 2.2 collective-permute-done.22
  110.5 6.6 %collective-permute-done.13 = bf16[128,1024]{1,0:T(8,128)(2,1)S(1)} collective-permute-done((bf16[128,1024]{1,0:T(8,128)(2,1)S(1)}, bf16[128,1024]{1,0:T(8,128)(2,1)S(1)}, u32[]{:S(2)}, u32[]{:S(2)}) %collective-permute-start.13) | collective-permute-done | bytes 262176 | tf_op jit(solution)/shard_map/ppermute | solution.py:483
  118.9 5.0 %collective-permute-done.14 = bf16[128,1024]{1,0:T(8,128)(2,1)S(1)} collective-permute-done((bf16[128,1024]{1,0:T(8,128)(2,1)S(1)}, bf16[128,1024]{1,0:T(8,128)(2,1)S(1)}, u32[]{:S(2)}, u32[]{:S(2)}) %collective-permute-start.14) | collective-permute-done | bytes 262176 | tf_op jit(solution)/shard_map/ppermute | solution.py:483
  135.7 5.3 %collective-permute-done.44 = bf16[64,2304]{1,0:T(8,128)(2,1)S(1)} collective-permute-done((bf16[64,2304]{1,0:T(8,128)(2,1)S(1)}, bf16[64,2304]{1,0:T(8,128)(2,1)S(1)}, u32[]{:S(2)}, u32[]{:S(2)}) %collective-permute-start.44) | collective-permute-done | bytes 294944 | tf_op jit(solution)/shard_map/ppermute | solution.py:558
  147.4 5.5 %collective-permute-done.27 = bf16[128,1024]{1,0:T(8,128)(2,1)S(1)} collective-permute-done((bf16[128,1024]{1,0:T(8,128)(2,1)S(1)}, bf16[128,1024]{1,0:T(8,128)(2,1)S(1)}, u32[]{:S(2)}, u32[]{:S(2)}) %collective-permute-start.27) | collective-permute-done | bytes 262176 | tf_op jit(solution)/shard_map/ppermute | solution.py:483
  153.9 3.5 %collective-permute-done.46 = bf16[128,2304]{1,0:T(8,128)(2,1)S(1)} collective-permute-done((bf16[128,2304]{1,0:T(8,128)(2,1)S(1)}, bf16[128,2304]{1,0:T(8,128)(2,1)S(1)}, u32[]{:S(2)}, u32[]{:S(2)}) %collective-permute-start.46) | collective-permute-done | bytes 589856 | tf_op jit(solution)/shard_map/ppermute | solution.py:558
  161.4 9.6 %collective-permute-done.48 = bf16[128,2304]{1,0:T(8,128)(2,1)S(1)} collective-permute-done((bf16[128,2304]{1,0:T(8,128)(2,1)S(1)}, bf16[128,2304]{1,0:T(8,128)(2,1)S(1)}, u32[]{:S(2)}, u32[]{:S(2)}) %collective-permute-start.48) | collective-permute-done | bytes 589856 | tf_op jit(solution)/shard_map/ppermute | solution.py:558
  176.1 7.1 %attend_back.1 = (bf16[512,1024]{1,0:T(8,128)(2,1)S(1)}, f32[8,128]{1,0:T(8,128)S(1)}) custom-call(f32[512,1024]{1,0:T(8,128)S(1)} %fusion.6.q_ref.k_ref.v_ref, f32[512,1024]{1,0:T(8,128)S(1)} %fusion.6.q_ref.k_ref.v_ref, f32[512,1024]{1,0:T(8,128)S(1)} %fusion.6.q_ref.k_ref.v_ref, bf16[512,512]{1,0:T(8,128)(2,1)S(1)} %attend.1.attn_ref, ...), custom_call_target="tpu_custom_call" | custom-call | tf_op jit(solution)/shard_map/attend_back/pallas_call | solution.py:412
  197.4 3.2 %collective-permute-done.32 = bf16[128,1536]{1,0:T(8,128)(2,1)S(1)} collective-permute-done((bf16[128,1536]{1,0:T(8,128)(2,1)S(1)}, bf16[128,1536]{1,0:T(8,128)(2,1)S(1)}, u32[]{:S(2)}, u32[]{:S(2)}) %collective-permute-start.32) | collective-permute-done | bytes 393248 | tf_op jit(solution)/shard_map/ppermute | solution.py:558
  210.8 3.3 %collective-permute-done.55 = f32[18,128]{1,0:T(8,128)S(1)} collective-permute-done((f32[18,128]{1,0:T(8,128)S(1)}, f32[18,128]{1,0:T(8,128)S(1)}, u32[]{:S(2)}, u32[]{:S(2)}) %collective-permute-start.55) | collective-permute-done | bytes 9248 | tf_op jit(solution)/shard_map/ppermute | solution.py:483
  215.7 2.1 collective-permute-done.56
  218.8 2.7 %collective-permute-done.57 = f32[18,128]{1,0:T(8,128)S(1)} collective-permute-done((f32[18,128]{1,0:T(8,128)S(1)}, f32[18,128]{1,0:T(8,128)S(1)}, u32[]{:S(2)}, u32[]{:S(2)}) %collective-permute-start.57) | collective-permute-done | bytes 9248 | tf_op jit(solution)/shard_map/ppermute | solution.py:648
  223.3 2.7 %collective-permute-done.58 = f32[18,128]{1,0:T(8,128)S(1)} collective-permute-done((f32[18,128]{1,0:T(8,128)S(1)}, f32[18,128]{1,0:T(8,128)S(1)}, u32[]{:S(2)}, u32[]{:S(2)}) %collective-permute-start.58) | collective-permute-done | bytes 9248 | tf_op jit(solution)/shard_map/ppermute | solution.py:648
  231.9 4.5 %collective-permute-done.35 = bf16[128,1024]{1,0:T(8,128)(2,1)S(1)} collective-permute-done((bf16[128,1024]{1,0:T(8,128)(2,1)S(1)}, bf16[128,1024]{1,0:T(8,128)(2,1)S(1)}, u32[]{:S(2)}, u32[]{:S(2)}) %collective-permute-start.35) | collective-permute-done | bytes 262176 | tf_op jit(solution)/shard_map/ppermute | solution.py:483
  238.6 5.2 %collective-permute-done.42 = bf16[2,32,1536]{2,1,0:T(8,128)(2,1)S(1)} collective-permute-done((bf16[2,32,1536]{2,1,0:T(8,128)(2,1)S(1)}, bf16[2,32,1536]{2,1,0:T(8,128)(2,1)S(1)}, u32[]{:S(2)}, u32[]{:S(2)}) %collective-permute-start.42) | collective-permute-done | bytes 196640 | tf_op jit(solution)/shard_map/ppermute | solution.py:483
  (348 shorter events, 111.3 us)
Async XLA Ops:
  10.6 27.0 %collective-permute-start = (bf16[128,2176]{1,0:T(8,128)(2,1)S(1)}, bf16[128,2176]{1,0:T(8,128)(2,1)S(1)}, u32[]{:S(2)}, u32[]{:S(2)}) collective-permute-start(bf16[128,2176]{1,0:T(8,128)(2,1)S(1)} %constant_dynamic-update-slice_fusion.9), channel_id=1, source_target_pairs={{0,2},{1,3},{2,0},{3,1},{4,6},{5,7},{6,4},{7,5},{8,10},{9,11},{10,... | collective-permute-start | bytes 1671176 | tf_op jit(solution)/shard_map/ppermute | solution.py:483
  14.0 17.0 %collective-permute-start.16 = (bf16[2,32,2304]{2,1,0:T(8,128)(2,1)S(1)}, bf16[2,32,2304]{2,1,0:T(8,128)(2,1)S(1)}, u32[]{:S(2)}, u32[]{:S(2)}) collective-permute-start(bf16[2,32,2304]{2,1,0:T(8,128)(2,1)S(1)} %get-tuple-element.133), channel_id=1, source_target_pairs={{0,2},{1,3},{2,0},{3,1},{4,6},{5,7},{6,4},{7,5},{8,10},{9,11},{10,... | collective-permute-start | bytes 884744 | tf_op jit(solution)/shard_map/ppermute | solution.py:483
  16.5 15.4 %collective-permute-start.3 = (bf16[2,32,1536]{2,1,0:T(8,128)(2,1)S(1)}, bf16[2,32,1536]{2,1,0:T(8,128)(2,1)S(1)}, u32[]{:S(2)}, u32[]{:S(2)}) collective-permute-start(bf16[2,32,1536]{2,1,0:T(8,128)(2,1)S(1)} %get-tuple-element.141), channel_id=1, source_target_pairs={{0,1},{1,0},{2,3},{3,2},{4,5},{5,4},{6,7},{7,6},{8,9},{9,8},{10,11... | collective-permute-start | bytes 589832 | tf_op jit(solution)/shard_map/ppermute | solution.py:483
  35.5 33.3 %collective-permute-start.18 = (bf16[128,2304]{1,0:T(8,128)(2,1)S(1)}, bf16[128,2304]{1,0:T(8,128)(2,1)S(1)}, u32[]{:S(2)}, u32[]{:S(2)}) collective-permute-start(bf16[128,2304]{1,0:T(8,128)(2,1)S(1)} %get-tuple-element.170), channel_id=1, source_target_pairs={{0,8},{1,9},{2,10},{3,11},{8,16},{9,17},{10,18},{11,19},{16,24},{1... | collective-permute-start | bytes 1769480 | tf_op jit(solution)/shard_map/ppermute | solution.py:558
  37.2 31.7 %collective-permute-start.19 = (bf16[128,2304]{1,0:T(8,128)(2,1)S(1)}, bf16[128,2304]{1,0:T(8,128)(2,1)S(1)}, u32[]{:S(2)}, u32[]{:S(2)}) collective-permute-start(bf16[128,2304]{1,0:T(8,128)(2,1)S(1)} %get-tuple-element.170), channel_id=1, source_target_pairs={{0,4},{1,5},{2,6},{3,7},{8,0},{9,1},{10,2},{11,3},{16,8},{17,9},{1... | collective-permute-start | bytes 1769480 | tf_op jit(solution)/shard_map/ppermute | solution.py:558
  37.7 33.4 %collective-permute-start.1 = (bf16[256,2176]{1,0:T(8,128)(2,1)S(1)}, bf16[256,2176]{1,0:T(8,128)(2,1)S(1)}, u32[]{:S(2)}, u32[]{:S(2)}) collective-permute-start(bf16[256,2176]{1,0:T(8,128)(2,1)S(1)} %pad_maximum_fusion.2), channel_id=1, source_target_pairs={{0,1},{1,0},{2,3},{3,2},{4,5},{5,4},{6,7},{7,6},{8,9},{9,8},{10,11... | collective-permute-start | bytes 3342344 | tf_op jit(solution)/shard_map/ppermute | solution.py:483
  46.5 19.0 %collective-permute-start.6 = (bf16[128,1536]{1,0:T(8,128)(2,1)S(1)}, bf16[128,1536]{1,0:T(8,128)(2,1)S(1)}, u32[]{:S(2)}, u32[]{:S(2)}) collective-permute-start(bf16[128,1536]{1,0:T(8,128)(2,1)S(1)} %collective-permute-done.4), channel_id=1, source_target_pairs={{0,8},{1,9},{2,10},{3,11},{8,16},{9,17},{10,18},{11,19},{16,24},{1... | collective-permute-start | bytes 1179656 | tf_op jit(solution)/shard_map/ppermute | solution.py:558
  48.1 18.8 %collective-permute-start.7 = (bf16[128,1536]{1,0:T(8,128)(2,1)S(1)}, bf16[128,1536]{1,0:T(8,128)(2,1)S(1)}, u32[]{:S(2)}, u32[]{:S(2)}) collective-permute-start(bf16[128,1536]{1,0:T(8,128)(2,1)S(1)} %collective-permute-done.5), channel_id=1, source_target_pairs={{0,4},{1,5},{2,6},{3,7},{8,0},{9,1},{10,2},{11,3},{16,8},{17,9},{1... | collective-permute-start | bytes 1179656 | tf_op jit(solution)/shard_map/ppermute | solution.py:558
  68.9 22.6 %collective-permute-start.20 = (bf16[128,2304]{1,0:T(8,128)(2,1)S(1)}, bf16[128,2304]{1,0:T(8,128)(2,1)S(1)}, u32[]{:S(2)}, u32[]{:S(2)}) collective-permute-start(bf16[128,2304]{1,0:T(8,128)(2,1)S(1)} %collective-permute-done.18), channel_id=1, source_target_pairs={{0,8},{1,9},{2,10},{3,11},{8,16},{9,17},{10,18},{11,19},{16,24},{1... | collective-permute-start | bytes 1769480 | tf_op jit(solution)/shard_map/ppermute | solution.py:558
  70.4 22.6 %collective-permute-start.21 = (bf16[128,2304]{1,0:T(8,128)(2,1)S(1)}, bf16[128,2304]{1,0:T(8,128)(2,1)S(1)}, u32[]{:S(2)}, u32[]{:S(2)}) collective-permute-start(bf16[128,2304]{1,0:T(8,128)(2,1)S(1)} %collective-permute-done.19), channel_id=1, source_target_pairs={{0,4},{1,5},{2,6},{3,7},{8,0},{9,1},{10,2},{11,3},{16,8},{17,9},{1... | collective-permute-start | bytes 1769480 | tf_op jit(solution)/shard_map/ppermute | solution.py:558
  80.4 15.3 %collective-permute-start.10 = (bf16[64,1536]{1,0:T(8,128)(2,1)S(1)}, bf16[64,1536]{1,0:T(8,128)(2,1)S(1)}, u32[]{:S(2)}, u32[]{:S(2)}) collective-permute-start(bf16[64,1536]{1,0:T(8,128)(2,1)S(1)} %slice.347), channel_id=1, source_target_pairs={{0,8},{1,9},{2,10},{3,11},{8,16},{9,17},{10,18},{11,19},{16,24},{1... | collective-permute-start | bytes 589832 | tf_op jit(solution)/shard_map/ppermute | solution.py:558
  82.0 15.2 %collective-permute-start.11 = (bf16[64,1536]{1,0:T(8,128)(2,1)S(1)}, bf16[64,1536]{1,0:T(8,128)(2,1)S(1)}, u32[]{:S(2)}, u32[]{:S(2)}) collective-permute-start(bf16[64,1536]{1,0:T(8,128)(2,1)S(1)} %slice.348), channel_id=1, source_target_pairs={{0,4},{1,5},{2,6},{3,7},{8,0},{9,1},{10,2},{11,3},{16,8},{17,9},{1... | collective-permute-start | bytes 589832 | tf_op jit(solution)/shard_map/ppermute | solution.py:558
  93.0 13.7 %collective-permute-start.22 = (bf16[128,2304]{1,0:T(8,128)(2,1)S(1)}, bf16[128,2304]{1,0:T(8,128)(2,1)S(1)}, u32[]{:S(2)}, u32[]{:S(2)}) collective-permute-start(bf16[128,2304]{1,0:T(8,128)(2,1)S(1)} %collective-permute-done.20), channel_id=1, source_target_pairs={{0,8},{1,9},{2,10},{3,11},{8,16},{9,17},{10,18},{11,19},{16,24},{1... | collective-permute-start | bytes 1769480 | tf_op jit(solution)/shard_map/ppermute | solution.py:558
  94.6 13.4 %collective-permute-start.23 = (bf16[128,2304]{1,0:T(8,128)(2,1)S(1)}, bf16[128,2304]{1,0:T(8,128)(2,1)S(1)}, u32[]{:S(2)}, u32[]{:S(2)}) collective-permute-start(bf16[128,2304]{1,0:T(8,128)(2,1)S(1)} %collective-permute-done.21), channel_id=1, source_target_pairs={{0,4},{1,5},{2,6},{3,7},{8,0},{9,1},{10,2},{11,3},{16,8},{17,9},{1... | collective-permute-start | bytes 1769480 | tf_op jit(solution)/shard_map/ppermute | solution.py:558
  108.0 16.0 %collective-permute-start.24 = (bf16[64,2304]{1,0:T(8,128)(2,1)S(1)}, bf16[64,2304]{1,0:T(8,128)(2,1)S(1)}, u32[]{:S(2)}, u32[]{:S(2)}) collective-permute-start(bf16[64,2304]{1,0:T(8,128)(2,1)S(1)} %slice.359), channel_id=1, source_target_pairs={{0,8},{1,9},{2,10},{3,11},{8,16},{9,17},{10,18},{11,19},{16,24},{1... | collective-permute-start | bytes 884744 | tf_op jit(solution)/shard_map/ppermute | solution.py:558
  143.1 14.3 %collective-permute-start.46 = (bf16[128,2304]{1,0:T(8,128)(2,1)S(1)}, bf16[128,2304]{1,0:T(8,128)(2,1)S(1)}, u32[]{:S(2)}, u32[]{:S(2)}) collective-permute-start(bf16[128,2304]{1,0:T(8,128)(2,1)S(1)} %pad_maximum_fusion.7), channel_id=1, source_target_pairs={{0,8},{1,9},{2,10},{3,11},{8,16},{9,17},{10,18},{11,19},{16,24},{1... | collective-permute-start | bytes 1769480 | tf_op jit(solution)/shard_map/ppermute | solution.py:558
  143.7 14.0 %collective-permute-start.47 = (bf16[128,2304]{1,0:T(8,128)(2,1)S(1)}, bf16[128,2304]{1,0:T(8,128)(2,1)S(1)}, u32[]{:S(2)}, u32[]{:S(2)}) collective-permute-start(bf16[128,2304]{1,0:T(8,128)(2,1)S(1)} %pad_maximum_fusion.8), channel_id=1, source_target_pairs={{0,4},{1,5},{2,6},{3,7},{8,0},{9,1},{10,2},{11,3},{16,8},{17,9},{1... | collective-permute-start | bytes 1769480 | tf_op jit(solution)/shard_map/ppermute | solution.py:558
  159.1 13.4 %collective-permute-start.49 = (bf16[128,2304]{1,0:T(8,128)(2,1)S(1)}, bf16[128,2304]{1,0:T(8,128)(2,1)S(1)}, u32[]{:S(2)}, u32[]{:S(2)}) collective-permute-start(bf16[128,2304]{1,0:T(8,128)(2,1)S(1)} %fusion.14), channel_id=1, source_target_pairs={{0,4},{1,5},{2,6},{3,7},{8,0},{9,1},{10,2},{11,3},{16,8},{17,9},{1... | collective-permute-start | bytes 1769480 | tf_op jit(solution)/shard_map/ppermute | solution.py:558
  161.3 14.0 %collective-permute-start.29 = (bf16[256,1024]{1,0:T(8,128)(2,1)S(1)}, bf16[256,1024]{1,0:T(8,128)(2,1)S(1)}, u32[]{:S(2)}, u32[]{:S(2)}) collective-permute-start(bf16[256,1024]{1,0:T(8,128)(2,1)S(1)} %pad_maximum_fusion.10), channel_id=1, source_target_pairs={{0,1},{1,0},{2,3},{3,2},{4,5},{5,4},{6,7},{7,6},{8,9},{9,8},{10,11... | collective-permute-start | bytes 1572872 | tf_op jit(solution)/shard_map/ppermute | solution.py:483
  172.6 22.2 %collective-permute-start.51 = (bf16[128,2304]{1,0:T(8,128)(2,1)S(1)}, bf16[128,2304]{1,0:T(8,128)(2,1)S(1)}, u32[]{:S(2)}, u32[]{:S(2)}) collective-permute-start(bf16[128,2304]{1,0:T(8,128)(2,1)S(1)} %fusion.16), channel_id=1, source_target_pairs={{0,4},{1,5},{2,6},{3,7},{8,0},{9,1},{10,2},{11,3},{16,8},{17,9},{1... | collective-permute-start | bytes 1769480 | tf_op jit(solution)/shard_map/ppermute | solution.py:558
  174.2 20.6 %collective-permute-start.50 = (bf16[128,2304]{1,0:T(8,128)(2,1)S(1)}, bf16[128,2304]{1,0:T(8,128)(2,1)S(1)}, u32[]{:S(2)}, u32[]{:S(2)}) collective-permute-start(bf16[128,2304]{1,0:T(8,128)(2,1)S(1)} %fusion.15), channel_id=1, source_target_pairs={{0,8},{1,9},{2,10},{3,11},{8,16},{9,17},{10,18},{11,19},{16,24},{1... | collective-permute-start | bytes 1769480 | tf_op jit(solution)/shard_map/ppermute | solution.py:558
  201.4 25.8 %collective-permute-start.38 = (bf16[128,1536]{1,0:T(8,128)(2,1)S(1)}, bf16[128,1536]{1,0:T(8,128)(2,1)S(1)}, u32[]{:S(2)}, u32[]{:S(2)}) collective-permute-start(bf16[128,1536]{1,0:T(8,128)(2,1)S(1)} %fusion.24), channel_id=1, source_target_pairs={{0,8},{1,9},{2,10},{3,11},{8,16},{9,17},{10,18},{11,19},{16,24},{1... | collective-permute-start | bytes 1179656 | tf_op jit(solution)/shard_map/ppermute | solution.py:558
  203.3 24.0 %collective-permute-start.39 = (bf16[128,1536]{1,0:T(8,128)(2,1)S(1)}, bf16[128,1536]{1,0:T(8,128)(2,1)S(1)}, u32[]{:S(2)}, u32[]{:S(2)}) collective-permute-start(bf16[128,1536]{1,0:T(8,128)(2,1)S(1)} %fusion.25), channel_id=1, source_target_pairs={{0,4},{1,5},{2,6},{3,7},{8,0},{9,1},{10,2},{11,3},{16,8},{17,9},{1... | collective-permute-start | bytes 1179656 | tf_op jit(solution)/shard_map/ppermute | solution.py:558
  205.1 24.6 %collective-permute-start.34 = (bf16[256,1024]{1,0:T(8,128)(2,1)S(1)}, bf16[256,1024]{1,0:T(8,128)(2,1)S(1)}, u32[]{:S(2)}, u32[]{:S(2)}) collective-permute-start(bf16[256,1024]{1,0:T(8,128)(2,1)S(1)} %slice.759), channel_id=1, source_target_pairs={{0,1},{1,0},{2,3},{3,2},{4,5},{5,4},{6,7},{7,6},{8,9},{9,8},{10,11... | collective-permute-start | bytes 1572872 | tf_op jit(solution)/shard_map/ppermute | solution.py:483
  (45 other events, 332.7 us)
